TPU v7x, 128 devices: a whole 4x4x4 slice. The times are simulated.
128 devices in a mesh: section: 4 (over z), dp: 32 (over y, x, core).
Axes of the slice: x: 4, y: 4, z: 4, core: 2. Of those that a mesh axis runs over, the one named last changes fastest.
Arguments:
- hidden: bfloat16 [64, 4, 8192], P('dp')
- delta: float32 [64, 8192], P('dp'), may hold values from -12 to 12
- gain: float32 [8192], replicated, may hold values from 0.5 to 1.5
- head: bfloat16 [131072, 8192], P(('section', 'dp'))
- targets: int32 [64, 3], replicated, may hold values from 0 to 131071
- tlen: int32 [64], replicated, may hold values from 1 to 3, as said below
Outputs:
- edit_loss: float32 [64], P('dp')
- value_step: float32 [64, 8192], P('dp')
Inputs may be any that keep to these rules, and one draw needn't show every extreme that they name: Entries of targets at positions tlen or later are not read.
All inputs are finite; a program needn't handle non-finite values.
Results may differ from a plain program's by a relative error of at most 0.0003.
The roundings to bfloat16 on the way count: a program that leaves them out, or rounds other values in their place, can miss the bound.
Values may be sent and summed in bfloat16 or wider, within the bound.
A program may use at most 128 MiB of HBM per device.

v0:
```python
import jax
import jax.numpy as jnp
from jax import lax
from jax.sharding import PartitionSpec as P

TGT = 3
EPS = 1e-05
KL_WEIGHT = 0.0625
STEP_RATE = 10.0


def normalize(values, gain):
    inv = lax.rsqrt(jnp.mean(values * values, axis=-1, keepdims=True) + EPS)
    return (values * inv * gain, inv)


def local(hidden, delta, gain, head, targets, tlen):
    edit_dev, slots, width = hidden.shape
    voc_dev = head.shape[0]
    edits = targets.shape[0]
    every = ("section", "dp")
    hid = hidden.astype(jnp.float32)
    shifted = hid + delta[:, None, :]
    normed, inv = normalize(shifted, gain)
    base, unused = normalize(hid[:, slots - 1, :], gain)
    rows = jnp.concatenate(
        [normed.astype(jnp.bfloat16), base.astype(jnp.bfloat16)[:, None, :]], axis=1
    )
    logits = lax.dot_general(
        lax.all_gather(rows, "dp", axis=0, tiled=True),
        head,
        (((2,), (1,)), ((), ())),
        preferred_element_type=jnp.float32,
    )
    local_top = jnp.max(logits, axis=-1)
    local_exp = jnp.exp(logits - local_top[:, :, None])
    local_total = jnp.sum(local_exp, axis=-1)
    gap = jnp.sum(local_exp[:, TGT + 1, :] * (logits[:, TGT + 1, :] - logits[:, TGT, :]), axis=-1)
    vocab_ids = lax.axis_index(every) * voc_dev + jnp.arange(voc_dev, dtype=jnp.int32)
    hit = targets[:, :, None] == vocab_ids[None, None, :]
    tgt_local = jnp.sum(jnp.where(hit, logits[:, :TGT, :], 0.0), axis=-1)
    packed = jnp.concatenate(
        [
            local_top.reshape(-1),
            local_total.reshape(-1),
            gap,
            tgt_local.reshape(-1),
            inv.reshape(-1),
        ]
    )
    every_stat = lax.all_gather(packed, every)
    n = edits * (TGT + 2)
    tops = every_stat[:, :n].reshape(-1, edits, TGT + 2)
    top = jnp.max(tops, axis=0)
    factor = jnp.exp(tops - top[None])
    total = jnp.sum(every_stat[:, n : 2 * n].reshape(-1, edits, TGT + 2) * factor, axis=0)
    gap_all = jnp.sum(every_stat[:, 2 * n : 2 * n + edits] * factor[:, :, TGT + 1], axis=0)
    first = 2 * n + edits
    tgt_sum = jnp.sum(every_stat[:, first : first + edits * TGT], axis=0).reshape(edits, TGT)
    dp = lax.axis_size("dp")
    inv_all = every_stat[:dp, first + edits * TGT :].reshape(edits, slots)
    logz = top + jnp.log(total)
    kl = gap_all / total[:, TGT + 1] - logz[:, TGT + 1] + logz[:, TGT]
    logp = logits - logz[:, :, None]
    tgt_logp = tgt_sum - logz[:, :TGT]
    lengths = tlen.astype(jnp.float32)
    weight = (jnp.arange(TGT, dtype=jnp.int32)[None, :] < tlen[:, None]).astype(
        jnp.float32
    ) / lengths[:, None]
    nll = -jnp.sum(tgt_logp * weight, axis=1)
    loss_all = nll + KL_WEIGHT * kl
    offset = lax.axis_index("dp") * edit_dev
    edit_loss = lax.dynamic_slice_in_dim(loss_all, offset, edit_dev, 0)
    probs = jnp.exp(logp)
    d_target = (probs[:, :TGT, :] - hit.astype(jnp.float32)) * weight[:, :, None]
    d_kl = KL_WEIGHT * (probs[:, TGT, :] - probs[:, TGT + 1, :])
    dlogits = jnp.concatenate([d_target, d_kl[:, None, :]], axis=1).astype(jnp.bfloat16)
    inner_local = jnp.sum(dlogits.astype(jnp.float32) * logits[:, :slots, :], axis=-1)
    gnorm = jnp.einsum("esv,vd->sed", dlogits, head, preferred_element_type=jnp.float32)
    mixed = jnp.sum(gnorm * inv_all.T[:, :, None], axis=0)
    full, inner = lax.psum((mixed, inner_local), every)
    mine = lax.dynamic_slice_in_dim(full, offset, edit_dev, 0)
    mine_inner = lax.dynamic_slice_in_dim(inner, offset, edit_dev, 0)[:, :, None]
    back = jnp.sum(shifted * (inv * inv * mine_inner / width), axis=1)
    value_step = -STEP_RATE * (gain * mine - back)
    return (edit_loss, value_step)


def solution(mesh):
    placed = (P("dp", None, None), P("dp", None), P(), P(("section", "dp"), None), P(), P())
    return jax.shard_map(
        local, mesh=mesh, in_specs=placed, out_specs=(P("dp"), P("dp", None)), check_vma=False
    )
```

profile of v0, /device:TPU:1, one launch (start us, length us, event | category | flops | bytes accessed | tf_op | source)
XLA Modules:
  0.0 408.3 jit_solution(15002139512185290136)
XLA Ops:
  7.2 0.9 convert_element_type.27
  8.1 0.2 multiply_reduce_fusion.2
  8.3 1.1 multiply_reduce_fusion.1
  9.4 0.1 copy.45
  9.5 0.1 copy.32
  9.6 0.9 multiply_convert_fusion.1
  10.5 1.1 multiply_convert_fusion
  11.6 0.8 pad_maximum_fusion.2
  12.6 56.3 %all-gather.3.cloned.1.call-done = bf16[64,5,8192]{2,1,0:T(8,128)(2,1)} async-done(((bf16[2,5,8192]{2,1,0:T(8,128)(2,1)}), bf16[64,5,8192]{2,1,0:T(8,128)(2,1)}) %all-gather.3.cloned.1.call-update) | async-done | bytes 5242896 | tf_op jit(solution)/shard_map/all_gather | solution.py:30
  68.9 15.8 %fusion.30 = (f32[64,5]{0,1:T(8,128)S(1)}, f32[64,5,1024]{2,0,1:T(8,128)S(1)}) fusion(bf16[1024,8192]{1,0:T(8,128)(2,1)} %param.9, bf16[64,5,8192]{2,1,0:T(8,128)(2,1)} %all-gather.3.cloned.1.call-done), kind=kOutput, calls=%fused_computation.55 | convolution fusion | flops 5369036288 | bytes 23332096 | tf_op jit(solution)/shard_map/dot_general | solution.py:29
  84.7 0.1 copy.34
  84.8 0.3 fusion.28
  85.1 0.1 fusion.22
  85.2 0.1 copy.35
  85.3 0.1 reshape.129
  85.5 0.2 fusion.15
  85.7 0.1 copy.36
  85.8 0.1 reshape.130
  86.0 0.1 reshape.128
  86.2 0.3 dynamic-update-slice
  86.5 0.8 copy-done.1
  87.3 0.2 all-reduce.4.cloned.1.call-start
  87.6 145.2 %all-reduce.6.cloned.1.call-done = f32[115712]{0:T(1024)} async-done(((f32[115712]{0:T(1024)}), f32[115712]{0:T(1024)}) %all-reduce.6.cloned.1.call-update) | async-done | bytes 462864
  232.8 1.5 reshape.134
  234.3 0.7 fusion.29
  235.0 0.1 fusion.23
  235.2 0.1 reduce_max.22
  235.3 0.1 slice_reduce_fusion
  235.4 0.1 reduce_sum.117
  235.6 0.3 copy-done.9
  235.9 0.3 copy-done.7
  236.2 0.3 subtract_exponential_fusion
  236.5 0.1 reshape.131
  236.7 0.7 convert_divide_fusion
  237.4 0.7 copy.42
  238.0 0.7 fusion.20
  238.7 0.9 fusion.18
  239.8 11.8 %fusion.11 = f32[64,8192]{1,0:T(8,128)} fusion(f32[4,64]{1,0:T(4,128)S(1)} %copy.43, bf16[1024,8192]{1,0:T(8,128)(2,1)} %param.9, bf16[64,1,1024]{2,0,1:T(8,128)(2,1)} %fusion.20, bf16[64,3,1024]{2,0,1:T(8,128)(2,1)S(1)} %fusion.18), kind=kOutput, calls=%fused_computation.7 | convolution fusion | flops 4298899456 | bytes 19399680 | tf_op jit(solution)/shard_map/esv,vd->sed/dot_general | solution.py:79
  251.7 0.7 copy-done.10
  252.5 0.2 fusion.14
  252.7 63.7 %psum.15 = f32[64,4]{0,1:T(4,128)S(1)} all-reduce(f32[64,4]{0,1:T(4,128)S(1)} %fusion.14), channel_id=1, replica_groups=mesh['section'=4,'dp'=32] {'section','dp'}, use_global_device_ids=true, to_apply=%region_14.15 | all-reduce | flops 256 | bytes 2048 | tf_op jit(solution)/shard_map/psum | solution.py:81
  316.5 0.1 copy.44
  316.7 0.1 copy.38
  317.0 0.2 slice_reduce_fusion.2
  317.3 0.6 dynamic_slice.9
  317.9 0.2 multiply_reduce_fusion
  318.1 82.0 %all-reduce.4.cloned.1.call-done = f32[64,8192]{1,0:T(8,128)} async-done(((f32[64,8192]{1,0:T(8,128)}), f32[64,8192]{1,0:T(8,128)}) %all-reduce.4.cloned.1.call-update) | async-done | bytes 2097168 | tf_op jit(solution)/shard_map/psum | solution.py:81
  400.1 1.6 subtract_multiply_fusion
  (57 shorter events, 1.2 us)
Async XLA Ops:
  7.2 61.7 %all-gather.3.cloned.1.call-start = ((), (), s32[]{:S(2)}) async-start(), calls=%async_computation | async-start | bytes 8650752 | tf_op jit(solution)/shard_map/all_gather | solution.py:30
  9.5 3.1 copy-start.13
  12.5 220.4 %all-reduce.6.cloned.1.call-start = ((), (), s32[]{:S(2)}) async-start(), calls=%async_computation.2 | async-start | bytes 925696
  12.6 72.9 %copy-start.12 = (s32[1024]{0:T(1024)}, s32[1024]{0:T(1024)S(1)}, u32[]{:S(2)}) copy-start(s32[1024]{0:T(1024)S(1)} %iota_add_fusion) | copy-start | bytes 12292
  84.7 0.8 copy-start.15
  84.8 2.8 copy-start.17
  86.5 0.8 copy-start.1
  87.3 312.8 %all-reduce.4.cloned.1.call-start = ((), (), s32[]{:S(2)}) async-start(), calls=%async_computation.1 | async-start | bytes 4194304 | tf_op jit(solution)/shard_map/psum | solution.py:81
  235.3 0.6 copy-start.9
  235.6 0.6 copy-start.7
  236.2 1.9 copy-start.2
  251.6 0.8 copy-start.10
  251.6 0.9 copy-start.6
  251.6 64.8 %copy-start.14 = (f32[2,4]{0,1:T(4,128)S(1)}, f32[2,4]{0,1:T(4,128)}, u32[]{:S(2)}) copy-start(f32[2,4]{0,1:T(4,128)} %copy-done.13) | copy-start | bytes 100
  251.6 65.1 %copy-start.4 = (f32[128,320]{1,0:T(8,128)S(1)}, f32[128,320]{1,0:T(8,128)}, u32[]{:S(2)}) copy-start(f32[128,320]{1,0:T(8,128)} %get-tuple-element.6) | copy-start | bytes 491524
  251.6 65.4 %copy-start.3 = (f32[64,5]{1,0:T(8,128)S(1)}, f32[64,5]{1,0:T(8,128)}, u32[]{:S(2)}) copy-start(f32[64,5]{1,0:T(8,128)} %copy-done.2) | copy-start | bytes 3844
  251.6 65.4 %copy-start.8 = (f32[64,5]{1,0:T(8,128)S(1)}, f32[64,5]{1,0:T(8,128)}, u32[]{:S(2)}) copy-start(f32[64,5]{1,0:T(8,128)} %copy-done.7) | copy-start | bytes 3844
  251.6 65.6 %copy-start.16 = (f32[64]{0:T(128)S(1)}, f32[64]{0:T(128)}, u32[]{:S(2)}) copy-start(f32[64]{0:T(128)} %get-tuple-element.9) | copy-start | bytes 772
  251.6 66.2 %copy-start = (bf16[2,4,8192]{2,1,0:T(4,128)(2,1)S(1)}, bf16[2,4,8192]{2,1,0:T(4,128)(2,1)}, u32[]{:S(2)}) copy-start(bf16[2,4,8192]{2,1,0:T(4,128)(2,1)} %param.6) | copy-start | bytes 393220
  251.6 66.2 %copy-start.5 = (f32[2,8192]{1,0:T(2,128)S(1)}, f32[2,8192]{1,0:T(2,128)}, u32[]{:S(2)}) copy-start(f32[2,8192]{1,0:T(2,128)} %param.7) | copy-start | bytes 196612
  251.7 148.5 %copy-start.11 = (f32[8192]{0:T(1024)S(1)}, f32[8192]{0:T(1024)}, u32[]{:S(2)}) copy-start(f32[8192]{0:T(1024)} %param.8) | copy-start | bytes 98308
Sparse Core Ops, SparseCore 0:
  12.6 56.2 all-gather.2
  87.5 145.3 all-reduce.5
  251.8 148.2 all-reduce.3
where the time goes:
time: 409 us; the launch traced here: 408 us
  waiting for transfers between devices  284 us (69%)
  blocking collectives  63.7 us (16%)
  matrix products  27.6 us (7%)
  between operations  14 us (3%)
  other arithmetic  11.4 us (3%)
  local copies, waits for them, and re-layouts  7.68 us (2%)
    unnamed x4, waiting for transfers between devices  145 us
    psum x1, waiting for transfers between devices, local(): full, inner = lax.psum((mixed, inner_local), every)  82 us
    psum x1, blocking collectives, local(): full, inner = lax.psum((mixed, inner_local), every)  63.7 us
    all_gather x1, waiting for transfers between devices, local(): lax.all_gather(rows, 'dp', axis=0, tiled=True)  56.3 us
    dot_general x1, matrix products, local(): lax.dot_general(lax.all_gather(rows, 'dp', axis=0, tiled=True), head, (((...  15.8 us
    dot_general x1, matrix products, local(): jnp.einsum('esv,vd->sed', dlogits, head, preferred_element_type=jnp.float32)  11.8 us
  transfers between devices with their start and end apart: 3, of which 3 were waited for; matrix products, arithmetic and copies ran while one was open for 0% of the time, Pallas kernels for 0%

commit v1 on v0

--- a/solution.py
+++ b/solution.py
@@ -27,7 +27,9 @@
         [normed.astype(jnp.bfloat16), base.astype(jnp.bfloat16)[:, None, :]], axis=1
     )
     logits = lax.dot_general(
-        lax.all_gather(rows, "dp", axis=0, tiled=True),
+        jnp.concatenate(
+            lax.all_to_all(jnp.stack([rows] * lax.axis_size("dp")), "dp", 0, 0), axis=0
+        ),
         head,
         (((2,), (1,)), ((), ())),
         preferred_element_type=jnp.float32,

time: 409 us -> 451 us (1.10)
  local copies, waits for them, and re-layouts: 7.68 us -> 38.9 us
  starting transfers between devices: 0.3 us -> 9.11 us
  waiting for transfers between devices: 284 us -> 290 us
  matrix products: 27.6 us -> 22.7 us
    all_to_all x0 -> x1, waiting for transfers between devices: none -> 61.6 us  [local(): lax.all_to_all(jnp.stack([rows] * lax.axis_size('dp')), 'dp', 0, 0)]
    all_gather x1 -> x0, waiting for transfers between devices: 56.3 us -> none  [local(): lax.all_gather(rows, 'dp', axis=0, tiled=True)]
    all_to_all x0 -> x1, local copies, waits for them, and re-layouts: none -> 14.4 us  [local(): lax.all_to_all(jnp.stack([rows] * lax.axis_size('dp')), 'dp', 0, 0)]
    reshape x0 -> x1, local copies, waits for them, and re-layouts: none -> 8.69 us  [local(): jnp.concatenate(lax.all_to_all(jnp.stack([rows] * lax.axis_size('dp')), '...]
    all_to_all x0 -> x1, starting transfers between devices: none -> 8.62 us  [local(): lax.all_to_all(jnp.stack([rows] * lax.axis_size('dp')), 'dp', 0, 0)]
    another operation x0 -> x1, local copies, waits for them, and re-layouts: none -> 7.61 us  [local(): jnp.stack([rows] * lax.axis_size('dp'))]
    dot_general x1, matrix products: 15.8 us -> 10.8 us  [local(): lax.dot_general(jnp.concatenate(lax.all_to_all(jnp.stack([rows] * lax.axi...]
    unnamed x4 -> x3, waiting for transfers between devices: 145 us -> 147 us
where the time goes in v1:
time: 451 us; the launch traced here: 450 us
  waiting for transfers between devices  290 us (64%)
  blocking collectives  64.2 us (14%)
  local copies, waits for them, and re-layouts  38.9 us (9%)
  matrix products  22.7 us (5%)
  between operations  14.4 us (3%)
  other arithmetic  10.6 us (2%)
  starting transfers between devices  9.11 us (2%)
    unnamed x3, waiting for transfers between devices  147 us
    psum x1, waiting for transfers between devices, local(): full, inner = lax.psum((mixed, inner_local), every)  81.5 us
    psum x1, blocking collectives, local(): full, inner = lax.psum((mixed, inner_local), every)  64.2 us
    all_to_all x1, waiting for transfers between devices, local(): lax.all_to_all(jnp.stack([rows] * lax.axis_size('dp')), 'dp', 0, 0)  61.6 us
    all_to_all x1, local copies, waits for them, and re-layouts, local(): lax.all_to_all(jnp.stack([rows] * lax.axis_size('dp')), 'dp', 0, 0)  14.4 us
    dot_general x1, matrix products, local(): jnp.einsum('esv,vd->sed', dlogits, head, preferred_element_type=jnp.float32)  11.8 us
    dot_general x1, matrix products, local(): lax.dot_general(jnp.concatenate(lax.all_to_all(jnp.stack([rows] * lax.axi...  10.8 us
  transfers between devices with their start and end apart: 3, of which 3 were waited for; matrix products, arithmetic and copies ran while one was open for 0% of the time, Pallas kernels for 0%

profile of v1, /device:TPU:1, one launch (start us, length us, event | category | flops | bytes accessed | tf_op | source)
XLA Modules:
  0.0 450.2 jit_solution(5405288272446656469)
XLA Ops:
  7.2 0.9 convert_element_type.27
  8.1 0.2 multiply_reduce_fusion.2
  8.3 1.1 multiply_reduce_fusion.1
  9.4 0.5 copy-done.13
  9.9 0.9 multiply_convert_fusion.1
  10.8 1.1 multiply_convert_fusion
  11.9 0.1 pad_maximum_fusion.2
  12.0 0.2 copy.39
  12.2 7.6 %stack.2 = bf16[32,2,5,8192]{3,1,2,0:T(2,128)(2,1)} broadcast(bf16[2,5,8192]{2,0,1:T(2,128)(2,1)S(1)} %copy.39), dimensions={1,2,3} | broadcast | bytes 5406720 | tf_op jit(solution)/shard_map/stack | solution.py:31
  19.8 8.6 %all-to-all-start = ((bf16[32,2,5,8192]{3,1,2,0:T(2,128)(2,1)}), bf16[32,2,5,8192]{3,1,2,0:T(2,128)(2,1)}, u32[]{:S(2)}, u32[]{:S(2)}) async-start(bf16[32,2,5,8192]{3,1,2,0:T(2,128)(2,1)} %stack.2), calls=%async_computation | async-start | bytes 10485760 | tf_op jit(solution)/shard_map/all_to_all | solution.py:31
  28.4 0.2 all-reduce.6.cloned.1.call-start
  28.8 61.6 %all-to-all-done = bf16[32,2,5,8192]{3,1,2,0:T(2,128)(2,1)} async-done(((bf16[32,2,5,8192]{3,1,2,0:T(2,128)(2,1)}), bf16[32,2,5,8192]{3,1,2,0:T(2,128)(2,1)}, u32[]{:S(2)}, u32[]{:S(2)}) %all-to-all-start) | async-done | bytes 5242912 | tf_op jit(solution)/shard_map/all_to_all | solution.py:31
  90.3 14.4 %copy.40 = bf16[32,2,5,8192]{3,1,0,2:T(2,128)(2,1)} copy(bf16[32,2,5,8192]{3,1,2,0:T(2,128)(2,1)} %all-to-all-done) | data formatting | bytes 10485760 | tf_op jit(solution)/shard_map/all_to_all | solution.py:31
  104.7 8.7 %reshape.133 = bf16[64,5,8192]{2,0,1:T(8,128)(2,1)} reshape(bf16[32,2,5,8192]{3,1,0,2:T(2,128)(2,1)} %copy.40) | data formatting | bytes 10485760 | tf_op jit(solution)/shard_map/reshape | solution.py:30
  113.4 10.8 %fusion.29 = (f32[64,5]{0,1:T(8,128)S(1)}, f32[64,5,1024]{2,0,1:T(8,128)S(1)}) fusion(bf16[64,5,8192]{2,0,1:T(8,128)(2,1)} %reshape.133, bf16[1024,8192]{1,0:T(8,128)(2,1)} %param.9), kind=kOutput, calls=%fused_computation.54 | convolution fusion | flops 5369036288 | bytes 23332096 | tf_op jit(solution)/shard_map/dot_general | solution.py:29
  124.4 0.3 fusion.27
  124.7 0.1 fusion.21
  125.0 0.1 reshape.135
  125.1 0.2 fusion.14
  125.4 0.1 reshape.136
  125.6 0.1 reshape.134
  125.9 0.3 dynamic-update-slice
  126.2 0.8 copy-done.1
  127.0 0.3 all-reduce.4.cloned.1.call-start
  127.3 147.2 %all-reduce.6.cloned.1.call-done = f32[115712]{0:T(1024)} async-done(((f32[115712]{0:T(1024)}), f32[115712]{0:T(1024)}) %all-reduce.6.cloned.1.call-update) | async-done | bytes 462864
  274.5 1.5 reshape.140
  276.0 0.7 fusion.28
  276.7 0.1 fusion.22
  276.8 0.1 reduce_max.22
  277.1 0.1 reduce_sum.117
  277.3 0.3 copy-done.9
  277.6 0.3 copy-done.7
  277.9 0.3 subtract_exponential_fusion
  278.2 0.1 reshape.137
  278.3 0.7 convert_divide_fusion
  279.1 0.7 copy.48
  279.7 0.7 fusion.19
  280.4 0.9 fusion.17
  281.4 11.8 %fusion.10 = f32[64,8192]{1,0:T(8,128)} fusion(f32[4,64]{1,0:T(4,128)S(1)} %copy.49, bf16[1024,8192]{1,0:T(8,128)(2,1)} %param.9, bf16[64,1,1024]{2,0,1:T(8,128)(2,1)} %fusion.19, bf16[64,3,1024]{2,0,1:T(8,128)(2,1)S(1)} %fusion.17), kind=kOutput, calls=%fused_computation.6 | convolution fusion | flops 4298899456 | bytes 19399680 | tf_op jit(solution)/shard_map/esv,vd->sed/dot_general | solution.py:81
  293.4 0.7 copy-done.10
  294.2 0.2 fusion.13
  294.6 0.1 copy.44
  294.9 0.2 slice_reduce_fusion.2
  295.2 0.6 dynamic_slice.9
  295.8 64.2 %psum.15 = f32[64,4]{1,0:T(8,128)S(1)} all-reduce(f32[64,4]{1,0:T(8,128)S(1)} %copy.50), channel_id=1, replica_groups=mesh['section'=4,'dp'=32] {'section','dp'}, use_global_device_ids=true, to_apply=%region_14.15 | all-reduce | flops 256 | bytes 2048 | tf_op jit(solution)/shard_map/psum | solution.py:83
  360.0 0.2 multiply_reduce_fusion
  360.2 81.5 %all-reduce.4.cloned.1.call-done = f32[64,8192]{1,0:T(8,128)} async-done(((f32[64,8192]{1,0:T(8,128)}), f32[64,8192]{1,0:T(8,128)}) %all-reduce.4.cloned.1.call-update) | async-done | bytes 2097168 | tf_op jit(solution)/shard_map/psum | solution.py:83
  441.7 1.6 subtract_multiply_fusion
  (58 shorter events, 1.5 us)
Async XLA Ops:
  9.4 0.5 copy-start.13
  19.8 70.5 %all-to-all-start = ((bf16[32,2,5,8192]{3,1,2,0:T(2,128)(2,1)}), bf16[32,2,5,8192]{3,1,2,0:T(2,128)(2,1)}, u32[]{:S(2)}, u32[]{:S(2)}) async-start(bf16[32,2,5,8192]{3,1,2,0:T(2,128)(2,1)} %stack.2), calls=%async_computation | async-start | bytes 10485760 | tf_op jit(solution)/shard_map/all_to_all | solution.py:31
  28.4 246.1 %all-reduce.6.cloned.1.call-start = ((), (), s32[]{:S(2)}) async-start(), calls=%async_computation.2 | async-start | bytes 925696
  28.8 96.3 %copy-start.12 = (s32[1024]{0:T(1024)}, s32[1024]{0:T(1024)S(1)}, u32[]{:S(2)}) copy-start(s32[1024]{0:T(1024)S(1)} %iota_add_fusion) | copy-start | bytes 12292
  124.3 0.8 copy-start.15
  124.4 2.9 copy-start.17
  126.2 0.8 copy-start.1
  127.0 314.7 %all-reduce.4.cloned.1.call-start = ((), (), s32[]{:S(2)}) async-start(), calls=%async_computation.1 | async-start | bytes 4194304 | tf_op jit(solution)/shard_map/psum | solution.py:83
  277.0 0.6 copy-start.9
  277.2 0.6 copy-start.7
  277.9 1.9 copy-start.2
  293.3 0.8 copy-start.10
  293.3 0.9 copy-start.6
  293.3 1.3 copy-start.4
  293.3 1.6 copy-start.3
  293.3 1.6 copy-start.8
  293.3 1.9 copy-start.16
  293.3 66.6 %copy-start.14 = (f32[2,4]{1,0:T(2,128)S(1)}, f32[2,4]{1,0:T(2,128)}, u32[]{:S(2)}) copy-start(f32[2,4]{1,0:T(2,128)} %copy-done.13) | copy-start | bytes 100
  293.3 66.6 %copy-start = (bf16[2,4,8192]{2,1,0:T(4,128)(2,1)S(1)}, bf16[2,4,8192]{2,1,0:T(4,128)(2,1)}, u32[]{:S(2)}) copy-start(bf16[2,4,8192]{2,1,0:T(4,128)(2,1)} %param.6) | copy-start | bytes 393220
  293.3 66.6 %copy-start.5 = (f32[2,8192]{1,0:T(2,128)S(1)}, f32[2,8192]{1,0:T(2,128)}, u32[]{:S(2)}) copy-start(f32[2,8192]{1,0:T(2,128)} %param.7) | copy-start | bytes 196612
  293.4 148.3 %copy-start.11 = (f32[8192]{0:T(1024)S(1)}, f32[8192]{0:T(1024)}, u32[]{:S(2)}) copy-start(f32[8192]{0:T(1024)} %param.8) | copy-start | bytes 98308
Sparse Core Ops, SparseCore 0:
  127.1 147.3 all-reduce.5
  293.5 148.1 all-reduce.3
